TPU v7x, 32 devices: a whole 2x2x4 slice. The times are simulated.
32 devices in a mesh: ctx: 4 (over y, x), wsh: 8 (over z, core).
Axes of the slice: x: 2, y: 2, z: 4, core: 2. Of those that a mesh axis runs over, the one named last changes fastest.
Arguments:
- tokens: bfloat16 [8, 2048, 768], P('wsh', 'ctx'), may hold values from -6 to 6
- cluster_order: int32 [8, 2048], P('wsh', 'ctx'), may hold values from 0 to 2047, as said below
- qkv_weight: bfloat16 [768, 2304], P('wsh'), may hold values from -0.21875 to 0.21875
- query_bias: bfloat16 [768], P('wsh'), may hold values from -3 to 3
- value_bias: bfloat16 [768], P('wsh'), may hold values from -1.25 to 1.25
- out_weight: bfloat16 [768, 768], P('wsh'), may hold values from -1.25 to 1.25
- out_bias: bfloat16 [768], P('wsh'), may hold values from -1.75 to 1.75
- first_gain: bfloat16 [768], P('wsh'), may hold values from 0.25 to 1.75
- first_shift: bfloat16 [768], P('wsh'), may hold values from -1.75 to 1.75
- up_weight: bfloat16 [768, 3072], P('wsh'), may hold values from -0.21875 to 0.21875
- up_bias: bfloat16 [3072], P('wsh'), may hold values from -3 to 3
- down_weight: bfloat16 [3072, 768], P('wsh'), may hold values from -0.109375 to 0.109375
- down_bias: bfloat16 [768], P('wsh'), may hold values from -1.75 to 1.75
- second_gain: bfloat16 [768], P('wsh'), may hold values from 0.25 to 1.75
- second_shift: bfloat16 [768], P('wsh'), may hold values from -1.75 to 1.75
- cotangent: bfloat16 [8, 2048, 768], P('wsh', 'ctx'), may hold values from -6 to 6
Outputs:
- layer_out: bfloat16 [8, 2048, 768], P('wsh', 'ctx')
- grad_tokens: float32 [8, 2048, 768], P('wsh', 'ctx')
- grad_qkv_weight: float32 [768, 2304], P('wsh')
- grad_query_bias: float32 [768], P('wsh')
- grad_value_bias: float32 [768], P('wsh')
- grad_out_weight: float32 [768, 768], P('wsh')
- grad_out_bias: float32 [768], P('wsh')
- grad_first_gain: float32 [768], P('wsh')
- grad_first_shift: float32 [768], P('wsh')
- grad_up_weight: float32 [768, 3072], P('wsh')
- grad_up_bias: float32 [3072], P('wsh')
- grad_down_weight: float32 [3072, 768], P('wsh')
- grad_down_bias: float32 [768], P('wsh')
- grad_second_gain: float32 [768], P('wsh')
- grad_second_shift: float32 [768], P('wsh')
Inputs may be any that keep to these rules, and one draw needn't show every extreme that they name: `cluster_order`: each stream's row is a permutation of its positions. The stream is cut into four documents, each a multiple of 128 tokens long, the longest exactly 1024; the permutation maps every document's positions onto themselves, so each cluster lies within one document.
All inputs are finite; a program needn't handle non-finite values.
Results may differ from a plain program's by a relative error of at most 0.02.
Values may be sent and summed in bfloat16 or wider, within the bound.
A program may use at most 128 MiB of HBM per device.

v0:
```python
import jax
import jax.numpy as jnp
from jax import lax
from jax.sharding import PartitionSpec as P

HEAD_DIM = 64
CLUSTER = 128
epsilon = 1e-05


def inner(left, right):
    return lax.dot_general(
        left, right, (((0,), (0,)), ((), ())), preferred_element_type=jnp.float32
    )


def times_transposed(left, right):
    return lax.dot_general(
        left, right, (((1,), (1,)), ((), ())), preferred_element_type=jnp.float32
    )


def normalize(values):
    centre = values - jnp.mean(values, axis=1, keepdims=True)
    factor = lax.rsqrt(jnp.mean(centre * centre, axis=1, keepdims=True) + epsilon)
    return (centre * factor, factor)


def norm_back(grad_out, normed, factor, gain):
    grad_normed = grad_out * gain
    return factor * (
        grad_normed
        - jnp.mean(grad_normed, axis=1, keepdims=True)
        - normed * jnp.mean(grad_normed * normed, axis=1, keepdims=True)
    )


def on_device(
    tokens,
    cluster_order,
    qkv_weight,
    query_bias,
    value_bias,
    out_weight,
    out_bias,
    first_gain,
    first_shift,
    up_weight,
    up_bias,
    down_weight,
    down_bias,
    second_gain,
    second_shift,
    cotangent,
):
    inputs = tokens[0]
    order = cluster_order[0]
    rows = inputs.shape[0]
    width = inputs.shape[1]
    heads = width // HEAD_DIM
    blocks = rows // CLUSTER
    group_rows = rows * lax.axis_size("ctx")
    factor_qk = HEAD_DIM ** (-0.5)
    (
        whole_qkv,
        whole_qbias,
        whole_vbias,
        whole_out,
        whole_obias,
        whole_gain1,
        whole_shift1,
        whole_up,
        whole_ubias,
        whole_down,
        whole_dbias,
        whole_gain2,
        whole_shift2,
    ) = (
        lax.all_gather(qkv_weight, "wsh", axis=0, tiled=True),
        lax.all_gather(query_bias, "wsh", axis=0, tiled=True),
        lax.all_gather(value_bias, "wsh", axis=0, tiled=True),
        lax.all_gather(out_weight, "wsh", axis=0, tiled=True),
        lax.all_gather(out_bias, "wsh", axis=0, tiled=True),
        lax.all_gather(first_gain, "wsh", axis=0, tiled=True),
        lax.all_gather(first_shift, "wsh", axis=0, tiled=True),
        lax.all_gather(up_weight, "wsh", axis=0, tiled=True),
        lax.all_gather(up_bias, "wsh", axis=0, tiled=True),
        lax.all_gather(down_weight, "wsh", axis=0, tiled=True),
        lax.all_gather(down_bias, "wsh", axis=0, tiled=True),
        lax.all_gather(second_gain, "wsh", axis=0, tiled=True),
        lax.all_gather(second_shift, "wsh", axis=0, tiled=True),
    )
    qkv_shift = jnp.concatenate(
        [
            whole_qbias.astype(jnp.float32),
            jnp.zeros((width,), jnp.float32),
            whole_vbias.astype(jnp.float32),
        ]
    )
    out_shift = whole_obias.astype(jnp.float32)
    gain_one = whole_gain1.astype(jnp.float32)
    shift_one = whole_shift1.astype(jnp.float32)
    up_shift = whole_ubias.astype(jnp.float32)
    down_shift = whole_dbias.astype(jnp.float32)
    gain_two = whole_gain2.astype(jnp.float32)
    shift_two = whole_shift2.astype(jnp.float32)
    own_qkv = (jnp.dot(inputs, whole_qkv, preferred_element_type=jnp.float32) + qkv_shift).astype(
        jnp.bfloat16
    )
    group_qkv = lax.all_gather(own_qkv, "ctx", axis=0, tiled=True)
    picked = jnp.take(group_qkv, order, axis=0)
    query = picked[:, :width].reshape(blocks, CLUSTER, heads, HEAD_DIM)
    keyed = picked[:, width : 2 * width].reshape(blocks, CLUSTER, heads, HEAD_DIM)
    valued = picked[:, 2 * width :].reshape(blocks, CLUSTER, heads, HEAD_DIM)
    places = order.reshape(blocks, CLUSTER)
    visible = (places[:, None, :] <= places[:, :, None])[:, None, :, :]
    scores = (
        jnp.einsum("cihd,cjhd->chij", query, keyed, preferred_element_type=jnp.float32) * factor_qk
    )
    masked = jnp.where(visible, scores, -1e30)
    row_max = jnp.max(masked, axis=3, keepdims=True)
    expd = jnp.where(visible, jnp.exp(masked - row_max), 0.0)
    total = jnp.sum(expd, axis=3, keepdims=True)
    log_total = row_max + jnp.log(total)
    probs = (expd / total).astype(jnp.bfloat16)
    context = (
        jnp.einsum("chij,cjhd->cihd", probs, valued, preferred_element_type=jnp.float32)
        .astype(jnp.bfloat16)
        .reshape(rows, width)
    )
    branch = (jnp.dot(context, whole_out, preferred_element_type=jnp.float32) + out_shift).astype(
        jnp.bfloat16
    )
    spread = jnp.zeros((group_rows, width), jnp.bfloat16).at[order].set(branch)
    attended = lax.psum_scatter(spread, "ctx", scatter_dimension=0, tiled=True).astype(jnp.float32)
    resid = inputs.astype(jnp.float32) + attended
    first_norm, first_factor = normalize(resid)
    first_out = first_norm * gain_one + shift_one
    first_low = first_out.astype(jnp.bfloat16)
    pre_act = jnp.dot(first_low, whole_up, preferred_element_type=jnp.float32) + up_shift
    hidden = jax.nn.gelu(pre_act, approximate=False).astype(jnp.bfloat16)
    second_in = (
        first_out + jnp.dot(hidden, whole_down, preferred_element_type=jnp.float32) + down_shift
    )
    second_norm, second_factor = normalize(second_in)
    layer_out = (second_norm * gain_two + shift_two).astype(jnp.bfloat16)
    grad_top = cotangent[0].astype(jnp.float32)
    grad_gain_two = jnp.sum(grad_top * second_norm, axis=0)
    grad_shift_two = jnp.sum(grad_top, axis=0)
    grad_second = norm_back(grad_top, second_norm, second_factor, gain_two)
    grad_branch2 = grad_second.astype(jnp.bfloat16)
    grad_down_w = inner(hidden, grad_branch2)
    grad_down_b = jnp.sum(grad_branch2.astype(jnp.float32), axis=0)
    grad_hidden = times_transposed(grad_branch2, whole_down)
    slope = (
        0.5 * (1.0 + lax.erf(pre_act * 0.7071067811865476))
        + pre_act * jnp.exp(-0.5 * pre_act * pre_act) * 0.3989422804014327
    )
    grad_pre = (grad_hidden * slope).astype(jnp.bfloat16)
    grad_up_w = inner(first_low, grad_pre)
    grad_up_b = jnp.sum(grad_pre.astype(jnp.float32), axis=0)
    grad_first = grad_second + times_transposed(grad_pre, whole_up)
    grad_gain_one = jnp.sum(grad_first * first_norm, axis=0)
    grad_shift_one = jnp.sum(grad_first, axis=0)
    grad_resid = norm_back(grad_first, first_norm, first_factor, gain_one)
    grad_attended = grad_resid.astype(jnp.bfloat16)
    grad_out_b = jnp.sum(grad_attended.astype(jnp.float32), axis=0)
    group_grads = lax.all_gather(grad_attended, "ctx", axis=0, tiled=True)
    picked_grad = jnp.take(group_grads, order, axis=0)
    grad_out_w = inner(context, picked_grad)
    grad_context = (
        times_transposed(picked_grad, whole_out)
        .astype(jnp.bfloat16)
        .reshape(blocks, CLUSTER, heads, HEAD_DIM)
    )
    again = (
        jnp.einsum("cihd,cjhd->chij", query, keyed, preferred_element_type=jnp.float32) * factor_qk
    )
    probs_full = jnp.where(visible, jnp.exp(jnp.where(visible, again, -1e30) - log_total), 0.0)
    probs_low = probs_full.astype(jnp.bfloat16)
    grad_probs = jnp.einsum(
        "cihd,cjhd->chij", grad_context, valued, preferred_element_type=jnp.float32
    )
    grad_valued = jnp.einsum(
        "chij,cihd->cjhd", probs_low, grad_context, preferred_element_type=jnp.float32
    ).astype(jnp.bfloat16)
    inner_sum = jnp.sum(probs_full * grad_probs, axis=3, keepdims=True)
    grad_scores = (probs_full * (grad_probs - inner_sum)).astype(jnp.bfloat16)
    grad_query = (
        jnp.einsum("chij,cjhd->cihd", grad_scores, keyed, preferred_element_type=jnp.float32)
        * factor_qk
    ).astype(jnp.bfloat16)
    grad_keyed = (
        jnp.einsum("chij,cihd->cjhd", grad_scores, query, preferred_element_type=jnp.float32)
        * factor_qk
    ).astype(jnp.bfloat16)
    grad_picked = jnp.concatenate(
        [
            grad_query.reshape(rows, width),
            grad_keyed.reshape(rows, width),
            grad_valued.reshape(rows, width),
        ],
        axis=1,
    )
    grad_query_b = jnp.sum(grad_picked[:, :width].astype(jnp.float32), axis=0)
    grad_value_b = jnp.sum(grad_picked[:, 2 * width :].astype(jnp.float32), axis=0)
    spread_grad = jnp.zeros((group_rows, 3 * width), jnp.bfloat16).at[order].set(grad_picked)
    own_grad = (
        lax.psum_scatter(spread_grad, "ctx", scatter_dimension=0, tiled=True)
        .astype(jnp.float32)
        .astype(jnp.bfloat16)
    )
    grad_qkv_w = inner(inputs, own_grad)
    grad_inputs = grad_resid + times_transposed(own_grad, whole_qkv)
    totals = (
        lax.psum_scatter(
            grad_qkv_w.astype(jnp.bfloat16), "wsh", scatter_dimension=0, tiled=True
        ).astype(jnp.float32),
        lax.psum_scatter(
            grad_query_b.astype(jnp.bfloat16), "wsh", scatter_dimension=0, tiled=True
        ).astype(jnp.float32),
        lax.psum_scatter(
            grad_value_b.astype(jnp.bfloat16), "wsh", scatter_dimension=0, tiled=True
        ).astype(jnp.float32),
        lax.psum_scatter(
            grad_out_w.astype(jnp.bfloat16), "wsh", scatter_dimension=0, tiled=True
        ).astype(jnp.float32),
        lax.psum_scatter(
            grad_out_b.astype(jnp.bfloat16), "wsh", scatter_dimension=0, tiled=True
        ).astype(jnp.float32),
        lax.psum_scatter(
            grad_gain_one.astype(jnp.bfloat16), "wsh", scatter_dimension=0, tiled=True
        ).astype(jnp.float32),
        lax.psum_scatter(
            grad_shift_one.astype(jnp.bfloat16), "wsh", scatter_dimension=0, tiled=True
        ).astype(jnp.float32),
        lax.psum_scatter(
            grad_up_w.astype(jnp.bfloat16), "wsh", scatter_dimension=0, tiled=True
        ).astype(jnp.float32),
        lax.psum_scatter(
            grad_up_b.astype(jnp.bfloat16), "wsh", scatter_dimension=0, tiled=True
        ).astype(jnp.float32),
        lax.psum_scatter(
            grad_down_w.astype(jnp.bfloat16), "wsh", scatter_dimension=0, tiled=True
        ).astype(jnp.float32),
        lax.psum_scatter(
            grad_down_b.astype(jnp.bfloat16), "wsh", scatter_dimension=0, tiled=True
        ).astype(jnp.float32),
        lax.psum_scatter(
            grad_gain_two.astype(jnp.bfloat16), "wsh", scatter_dimension=0, tiled=True
        ).astype(jnp.float32),
        lax.psum_scatter(
            grad_shift_two.astype(jnp.bfloat16), "wsh", scatter_dimension=0, tiled=True
        ).astype(jnp.float32),
    )
    (
        sum_qkv,
        sum_qbias,
        sum_vbias,
        sum_out,
        sum_obias,
        sum_gain1,
        sum_shift1,
        sum_up,
        sum_ubias,
        sum_down,
        sum_dbias,
        sum_gain2,
        sum_shift2,
    ) = (
        lax.psum(totals[0].astype(jnp.bfloat16), "ctx").astype(jnp.float32),
        lax.psum(totals[1].astype(jnp.bfloat16), "ctx").astype(jnp.float32),
        lax.psum(totals[2].astype(jnp.bfloat16), "ctx").astype(jnp.float32),
        lax.psum(totals[3].astype(jnp.bfloat16), "ctx").astype(jnp.float32),
        lax.psum(totals[4].astype(jnp.bfloat16), "ctx").astype(jnp.float32),
        lax.psum(totals[5].astype(jnp.bfloat16), "ctx").astype(jnp.float32),
        lax.psum(totals[6].astype(jnp.bfloat16), "ctx").astype(jnp.float32),
        lax.psum(totals[7].astype(jnp.bfloat16), "ctx").astype(jnp.float32),
        lax.psum(totals[8].astype(jnp.bfloat16), "ctx").astype(jnp.float32),
        lax.psum(totals[9].astype(jnp.bfloat16), "ctx").astype(jnp.float32),
        lax.psum(totals[10].astype(jnp.bfloat16), "ctx").astype(jnp.float32),
        lax.psum(totals[11].astype(jnp.bfloat16), "ctx").astype(jnp.float32),
        lax.psum(totals[12].astype(jnp.bfloat16), "ctx").astype(jnp.float32),
    )
    return (
        layer_out[None],
        grad_inputs[None],
        sum_qkv,
        sum_qbias,
        sum_vbias,
        sum_out,
        sum_obias,
        sum_gain1,
        sum_shift1,
        sum_up,
        sum_ubias,
        sum_down,
        sum_dbias,
        sum_gain2,
        sum_shift2,
    )


def solution(mesh):
    in_specs = (
        P("wsh", "ctx", None),
        P("wsh", "ctx"),
        P("wsh", None),
        P("wsh"),
        P("wsh"),
        P("wsh", None),
        P("wsh"),
        P("wsh"),
        P("wsh"),
        P("wsh", None),
        P("wsh"),
        P("wsh", None),
        P("wsh"),
        P("wsh"),
        P("wsh"),
        P("wsh", "ctx", None),
    )
    out_specs = (
        P("wsh", "ctx", None),
        P("wsh", "ctx", None),
        P("wsh", None),
        P("wsh"),
        P("wsh"),
        P("wsh", None),
        P("wsh"),
        P("wsh"),
        P("wsh"),
        P("wsh", None),
        P("wsh"),
        P("wsh", None),
        P("wsh"),
        P("wsh"),
        P("wsh"),
    )
    return jax.shard_map(
        on_device, mesh=mesh, in_specs=in_specs, out_specs=out_specs, check_vma=False
    )
```

profile of v0, /device:TPU:0, one launch (start us, length us, event | category | flops | bytes accessed | tf_op | source)
XLA Modules:
  0.0 820.0 jit_solution(3565493798486074965)
XLA Ops:
  8.0 1.3 fusion.86
  15.8 31.6 %all-reduce.18 = (bf16[768]{0:T(1024)(128)(2,1)S(1)}, bf16[768]{0:T(1024)(128)(2,1)S(1)}, bf16[768]{0:T(1024)(128)(2,1)S(1)}, bf16[768]{0:T(1024)(128)(2,1)S(1)}...) all-reduce(bf16[768]{0:T(1024)(128)(2,1)S(1)} %dynamic-update-slice, ...), channel_id=1, replica_groups=mesh['ctx'=4,'wsh'=8] {'wsh'}, use_global_device_ids=true, to_apply=%add.1 | all-reduce | flops 5376 | bytes 21504
  47.5 7.0 all-gather.8.cloned.1.call-done
  54.4 5.6 fusion.18
  61.1 94.4 %all-gather.10.cloned.1.call-done = bf16[2048,2304]{1,0:T(8,128)(2,1)} async-done(((bf16[512,2304]{1,0:T(8,128)(2,1)}), bf16[2048,2304]{1,0:T(8,128)(2,1)}) %all-gather.10.cloned.1.call-update) | async-done | bytes 9437200 | tf_op jit(solution)/shard_map/all_gather | solution.py:110
  155.5 10.8 %gather_fusion = bf16[512,2304]{1,0:T(8,128)(2,1)} fusion(bf16[2048,2304]{1,0:T(8,128)(2,1)} %all-gather.10.cloned.1.call-done, s32[1024]{0:T(1024)S(1)} %pad_clamp_fusion), kind=kCustom, calls=%fused_computation | custom fusion | bytes 4720640 | tf_op jit(solution)/shard_map/jit(_take)/gather | solution.py:111
  166.3 1.9 broadcast_select_fusion
  175.8 4.1 all-gather.12.cloned.1.call-done
  179.8 2.1 add_convert_fusion.1
  182.0 4.7 scatter_custom_fusion
  187.9 13.1 %all-gather = bf16[8,1,384]{2,1,0:T(2,128)(2,1)S(1)} all-gather(bf16[1,1,384]{2,1,0:T(2,128)(2,1)S(1)} %reshape.219), channel_id=1, replica_groups=mesh['ctx'=4,'wsh'=8] {'wsh'}, dimensions={0}, use_global_device_ids=true | all-gather | bytes 6912 | tf_op jit(solution)/shard_map/all_gather | solution.py:87
  201.1 29.5 %reduce-scatter.9.cloned.1.call-done = bf16[512,768]{1,0:T(8,128)(2,1)} async-done(((bf16[2048,768]{1,0:T(8,128)(2,1)}), bf16[512,768]{1,0:T(8,128)(2,1)}) %reduce-scatter.9.cloned.1.call-update) | async-done | bytes 786448 | tf_op jit(solution)/shard_map/reduce_scatter | solution.py:135
  230.6 1.5 fusion.36
  232.1 1.5 multiply_reduce_fusion.4
  233.6 50.2 %all-gather.14.cloned.1.call-done = bf16[768,3072]{1,0:T(8,128)(2,1)} async-done(((bf16[96,3072]{1,0:T(8,128)(2,1)}), bf16[768,3072]{1,0:T(8,128)(2,1)}) %all-gather.14.cloned.1.call-update) | async-done | bytes 4718608 | tf_op jit(solution)/shard_map/all_gather | solution.py:86
  283.8 19.3 %fusion.2 = (bf16[512,3072]{1,0:T(8,128)(2,1)}, f32[512,3072]{1,0:T(8,128)}) fusion(f32[3072]{0:T(1024)S(1)} %bitcast.121, bf16[768,3072]{1,0:T(8,128)(2,1)} %all-gather.14.cloned.1.call-done, f32[768]{0:T(1024)S(1)} %convert_element_type.212, f32[768]{0:T(1024)S(1)} %convert_element_type.211, f32[512]{0:T(512)S(1)} %add_rsqrt_fusion.1, ...), kind=kOutput, calls=%fused_computation.8 | convolution fusion | flops 2522873856 | bytes 15751168 | tf_op jit(solution)/shard_map/dot_general | solution.py:140
  303.1 32.7 %all-gather.16.cloned.1.call-done = bf16[3072,768]{1,0:T(8,128)(2,1)} async-done(((bf16[384,768]{1,0:T(8,128)(2,1)}), bf16[3072,768]{1,0:T(8,128)(2,1)}) %all-gather.16.cloned.1.call-update) | async-done | bytes 4718608 | tf_op jit(solution)/shard_map/all_gather | solution.py:88
  335.8 6.3 fusion.87
  344.8 4.7 fusion.90
  349.6 3.2 multiply_reduce_fusion.1
  354.0 1.5 fusion.83
  355.6 42.9 %all-gather.18.cloned.1.call-done = bf16[2048,768]{1,0:T(8,128)(2,1)} async-done(((bf16[512,768]{1,0:T(8,128)(2,1)}), bf16[2048,768]{1,0:T(8,128)(2,1)}) %all-gather.18.cloned.1.call-update) | async-done | bytes 3145744 | tf_op jit(solution)/shard_map/all_gather | solution.py:168
  398.5 5.5 gather_fusion.1
  404.0 3.2 convolution_convert_fusion.4
  407.2 2.3 copy.89
  409.5 2.4 reshape.158
  412.0 3.8 multiply_reduce_fusion
  422.9 1.7 pad_maximum_fusion
  424.6 4.3 copy.101
  428.9 10.7 %scatter_custom_fusion.1 = bf16[2048,2304]{1,0:T(8,128)(2,1)} fusion(s32[512]{0:T(512)S(1)} %bitcast.125, bf16[512,2304]{1,0:T(8,128)(2,1)} %copy.101, bf16[]{:T(256)} %constant.42.clone.1), kind=kCustom, calls=%fused_computation.34 | custom fusion | bytes 9437696 | tf_op jit(solution)/shard_map/scatter | solution.py:207
  439.7 95.1 %reduce-scatter.11.cloned.1.call-done = bf16[512,2304]{1,0:T(8,128)(2,1)} async-done(((bf16[2048,2304]{1,0:T(8,128)(2,1)}), bf16[512,2304]{1,0:T(8,128)(2,1)}) %reduce-scatter.11.cloned.1.call-update) | async-done | bytes 2359312 | tf_op jit(solution)/shard_map/reduce_scatter | solution.py:209
  534.8 5.5 fusion.19
  540.3 5.8 copy.107
  546.2 3.3 convolution_convert_fusion.3
  549.5 6.5 convolution_convert_fusion.1
  556.3 7.2 convolution_convert_fusion
  563.6 26.5 %reduce-scatter.19.cloned.1.call-done = bf16[96,2304]{1,0:T(8,128)(2,1)} async-done(((bf16[768,2304]{1,0:T(8,128)(2,1)}), bf16[96,2304]{1,0:T(8,128)(2,1)}) %reduce-scatter.19.cloned.1.call-update) | async-done | bytes 442384
  590.1 2.1 copy.108
  592.2 32.2 %reduce-scatter.13.cloned.1.call-done = bf16[96,768]{1,0:T(8,128)(2,1)} async-done(((bf16[768,768]{1,0:T(8,128)(2,1)}), bf16[96,768]{1,0:T(8,128)(2,1)}) %reduce-scatter.13.cloned.1.call-update) | async-done | bytes 147472 | tf_op jit(solution)/shard_map/reduce_scatter | solution.py:225
  624.3 55.5 %reduce-scatter.15.cloned.1.call-done = bf16[96,3072]{1,0:T(8,128)(2,1)} async-done(((bf16[768,3072]{1,0:T(8,128)(2,1)}), bf16[96,3072]{1,0:T(8,128)(2,1)}) %reduce-scatter.15.cloned.1.call-update) | async-done | bytes 589840 | tf_op jit(solution)/shard_map/reduce_scatter | solution.py:237
  679.8 55.6 %reduce-scatter.17.cloned.1.call-done = bf16[384,768]{1,0:T(8,128)(2,1)} async-done(((bf16[3072,768]{1,0:T(8,128)(2,1)}), bf16[384,768]{1,0:T(8,128)(2,1)}) %reduce-scatter.17.cloned.1.call-update) | async-done | bytes 589840 | tf_op jit(solution)/shard_map/reduce_scatter | solution.py:243
  738.4 26.0 %all-reduce.17 = (bf16[768]{0:T(1024)(128)(2,1)S(1)}, bf16[768]{0:T(1024)(128)(2,1)S(1)}, bf16[768]{0:T(1024)(128)(2,1)S(1)}, bf16[768]{0:T(1024)(128)(2,1)S(1)}...) all-reduce(bf16[768]{0:T(1024)(128)(2,1)S(1)} %dynamic-update-slice, ...), channel_id=1, replica_groups=mesh['ctx'=4,'wsh'=8] {'wsh'}, use_global_device_ids=true, to_apply=%add.7 | all-reduce | flops 9984 | bytes 39936
  765.1 9.9 %all-reduce.19 = (bf16[96]{0:T(256)(128)(2,1)S(1)}, bf16[96]{0:T(256)(128)(2,1)S(1)}, bf16[96]{0:T(256)(128)(2,1)S(1)}, bf16[96]{0:T(256)(128)(2,1)S(1)}, bf16[9...) all-reduce(bf16[96]{0:T(256)(128)(2,1)S(1)} %dynamic-slice.9, ...), channel_id=1, replica_groups=mesh['ctx'=4,'wsh'=8] {'ctx'}, use_global_device_ids=true, to_apply=%region_19.20 | all-reduce | flops 1152 | bytes 4608 | tf_op jit(solution)/shard_map/psum | solution.py:272
  780.9 6.4 add_bitcast_fusion
  787.3 18.7 %all-reduce.23.cloned.1.call-done = (bf16[96,2304]{0,1:T(8,128)(2,1)}, bf16[96,768]{1,0:T(8,128)(2,1)}, bf16[96,3072]{1,0:T(8,128)(2,1)}, bf16[384,768]{1,0:T(8,128)(2,1)}) async-done(((bf16[96,2304]{0,1:T(8,128)(2,1)}, bf16[96,768]{1,0:T(8,128)(2,1)}, bf16[96,3072]{1,0:T(8,128)(2,1)}, bf16[384,768]{1,0:T(8,128)(2,1)}), (bf16[96,2304]{0,1:T(8,128)(2,1)}, bf16[96,768]{1,0:T(8,128)(2,1)}, ...) | async-done | bytes 1769488 | tf_op jit(solution)/shard_map/psum | solution.py:271
  806.0 2.3 copy.102
  808.3 1.6 convert_element_type.240
  809.9 2.2 convert_element_type.247
  (160 shorter events, 37.1 us)
Async XLA Ops:
  7.2 47.3 %all-gather.8.cloned.1.call-start = ((), (), s32[]{:S(2)}) async-start(), calls=%async_computation.6 | async-start | bytes 3981312 | tf_op jit(solution)/shard_map/all_gather | solution.py:79
  7.9 147.6 %all-gather.10.cloned.1.call-start = ((), (), s32[]{:S(2)}) async-start(), calls=%async_computation.7 | async-start | bytes 11796480 | tf_op jit(solution)/shard_map/all_gather | solution.py:110
  47.5 13.4 %copy-start.15 = (s32[1,512]{1,0:T(1,128)S(1)}, s32[1,512]{1,0:T(1,128)}, u32[]{:S(2)}) copy-start(s32[1,512]{1,0:T(1,128)} %param.17) | copy-start | bytes 6148
  60.1 119.7 %all-gather.12.cloned.1.call-start = ((), (), s32[]{:S(2)}) async-start(), calls=%async_computation.8 | async-start | bytes 1327104 | tf_op jit(solution)/shard_map/all_gather | solution.py:82
  60.8 169.7 %reduce-scatter.9.cloned.1.call-start = ((), (), s32[]{:S(2)}) async-start(), calls=%async_computation.9 | async-start | bytes 3932160 | tf_op jit(solution)/shard_map/reduce_scatter | solution.py:135
  169.8 1.8 copy-start.5
  171.1 1.1 copy-start.7
  172.3 1.8 copy-start.12
  173.1 2.0 copy-start
  175.7 6.2 copy-start.11
  181.9 5.9 copy-start.16
  181.9 48.6 %copy-start.2 = (bf16[1,512,768]{2,1,0:T(8,128)(2,1)S(1)}, bf16[1,512,768]{2,1,0:T(8,128)(2,1)}, u32[]{:S(2)}) copy-start(bf16[1,512,768]{2,1,0:T(8,128)(2,1)} %param.16) | copy-start | bytes 2359300
  186.7 97.1 %all-gather.14.cloned.1.call-start = ((), (), s32[]{:S(2)}) async-start(), calls=%async_computation.10 | async-start | bytes 5308416 | tf_op jit(solution)/shard_map/all_gather | solution.py:86
  187.2 148.6 %all-gather.16.cloned.1.call-start = ((), (), s32[]{:S(2)}) async-start(), calls=%async_computation.11 | async-start | bytes 5308416 | tf_op jit(solution)/shard_map/all_gather | solution.py:88
  187.8 210.6 %all-gather.18.cloned.1.call-start = ((), (), s32[]{:S(2)}) async-start(), calls=%async_computation.12 | async-start | bytes 3932160 | tf_op jit(solution)/shard_map/all_gather | solution.py:168
  230.6 53.2 %copy-start.3 = (bf16[512,768]{1,0:T(8,128)(2,1)S(1)}, bf16[512,768]{1,0:T(8,128)(2,1)}, u32[]{:S(2)}) copy-start(bf16[512,768]{1,0:T(8,128)(2,1)} %reduce-scatter.9.cloned.1.call-done) | copy-start | bytes 2359300
  335.8 6.6 copy-start.4
  335.8 8.0 copy-start.20
  342.4 2.4 copy-start.17
  343.2 6.4 slice-start
  343.8 5.8 copy-start.10
  344.8 4.8 slice-start.1
  349.6 3.3 copy-start.19
  352.8 1.1 copy-start.9
  355.5 179.3 %reduce-scatter.11.cloned.1.call-start = ((), (), s32[]{:S(2)}) async-start(), calls=%async_computation.13 | async-start | bytes 11796480 | tf_op jit(solution)/shard_map/reduce_scatter | solution.py:209
  412.0 3.8 copy-start.1
  412.0 3.8 copy-start.13
  417.1 1.2 copy-start.6
  418.3 1.1 copy-start.8
  439.6 150.5 %reduce-scatter.19.cloned.1.call-start = ((), (), s32[]{:S(2)}) async-start(), calls=%async_computation.17 | async-start | bytes 3981312
  546.1 78.2 %reduce-scatter.13.cloned.1.call-start = ((), (), s32[]{:S(2)}) async-start(), calls=%async_computation.14 | async-start | bytes 1327104 | tf_op jit(solution)/shard_map/reduce_scatter | solution.py:225
  549.5 130.3 %reduce-scatter.15.cloned.1.call-start = ((), (), s32[]{:S(2)}) async-start(), calls=%async_computation.15 | async-start | bytes 5308416 | tf_op jit(solution)/shard_map/reduce_scatter | solution.py:237
  556.0 179.4 %reduce-scatter.17.cloned.1.call-start = ((), (), s32[]{:S(2)}) async-start(), calls=%async_computation.16 | async-start | bytes 5308416 | tf_op jit(solution)/shard_map/reduce_scatter | solution.py:243
  563.5 174.5 %copy-start.18 = (bf16[96]{0:T(256)(128)(2,1)S(1)}, bf16[96]{0:T(256)(128)(2,1)}, u32[]{:S(2)}) copy-start(bf16[96]{0:T(256)(128)(2,1)} %param.30) | copy-start | bytes 580
  563.5 242.5 %all-reduce.23.cloned.1.call-start = ((), (), s32[]{:S(2)}) async-start(), calls=%async_computation.18 | async-start | bytes 3833856 | tf_op jit(solution)/shard_map/psum | solution.py:271
  806.0 6.1 copy-start.14
Sparse Core Ops, SparseCore 0:
  9.7 44.7 all-gather.7
  60.2 95.2 all-gather.9
  157.1 22.6 all-gather.11
  186.8 43.7 reduce-scatter.8
  232.0 51.6 all-gather.13
  285.2 50.5 all-gather.15
  355.6 42.7 all-gather.17
  439.8 95.0 reduce-scatter.10
  546.2 43.8 reduce-scatter.18
  592.9 31.3 reduce-scatter.12
  626.8 52.9 reduce-scatter.14
  682.1 53.3 reduce-scatter.16
  739.9 66.0 all-reduce.22
where the time goes:
time: 825 us; the launch traced here: 820 us
  waiting for transfers between devices  547 us (66%)
  matrix products  82 us (10%)
  blocking collectives  80.7 us (10%)
  local copies, waits for them, and re-layouts  68.7 us (8%)
  other arithmetic  24.3 us (3%)
  between operations  16.7 us (2%)
    reduce_scatter x1, waiting for transfers between devices, on_device(): lax.psum_scatter(spread_grad, 'ctx', scatter_dimension=0, tiled=True)  95.1 us
    all_gather x1, waiting for transfers between devices, on_device(): group_qkv = lax.all_gather(own_qkv, 'ctx', axis=0, tiled=True)  94.4 us
    unnamed x2, blocking collectives  57.6 us
    reduce_scatter x1, waiting for transfers between devices, on_device(): lax.psum_scatter(grad_down_w.astype(jnp.bfloat16), 'wsh', scatter_dimensi...  55.6 us
    reduce_scatter x1, waiting for transfers between devices, on_device(): lax.psum_scatter(grad_up_w.astype(jnp.bfloat16), 'wsh', scatter_dimension...  55.5 us
    all_gather x1, waiting for transfers between devices, on_device(): lax.all_gather(up_weight, 'wsh', axis=0, tiled=True)  50.2 us
    all_gather x1, waiting for transfers between devices, on_device(): group_grads = lax.all_gather(grad_attended, 'ctx', axis=0, tiled=True)  42.9 us
    all_gather x1, waiting for transfers between devices, on_device(): lax.all_gather(down_weight, 'wsh', axis=0, tiled=True)  32.7 us
  transfers between devices with their start and end apart: 13, of which 13 were waited for; matrix products, arithmetic and copies ran while one was open for 10% of the time, Pallas kernels for 0%

commit v1 on v0

--- a/solution.py
+++ b/solution.py
@@ -107,7 +107,15 @@
     own_qkv = (jnp.dot(inputs, whole_qkv, preferred_element_type=jnp.float32) + qkv_shift).astype(
         jnp.bfloat16
     )
-    group_qkv = lax.all_gather(own_qkv, "ctx", axis=0, tiled=True)
+    n_shards = lax.axis_size("ctx")
+    ledger = [own_qkv]
+    for at in tuple(range(n_shards - 1)):
+        ledger.append(
+            lax.ppermute(ledger[-1], "ctx", [(no, (no + 1) % n_shards) for no in range(n_shards)])
+        )
+    group_qkv = jnp.roll(
+        jnp.concatenate(ledger[::-1], 0), (lax.axis_index("ctx") + 1) * own_qkv.shape[0], axis=0
+    )
     picked = jnp.take(group_qkv, order, axis=0)
     query = picked[:, :width].reshape(blocks, CLUSTER, heads, HEAD_DIM)
     keyed = picked[:, width : 2 * width].reshape(blocks, CLUSTER, heads, HEAD_DIM)

time: 825 us -> 911 us (1.10)
  waiting for transfers between devices: 547 us -> 604 us
  local copies, waits for them, and re-layouts: 68.7 us -> 95.1 us
    ppermute x0 -> x3, waiting for transfers between devices: none -> 158 us  [on_device(): lax.ppermute(ledger[-1], 'ctx', [(no, (no + 1) % n_shards) for no in rang...]
    all_gather x1 -> x0, waiting for transfers between devices: 94.4 us -> none  [on_device(): group_qkv = lax.all_gather(own_qkv, 'ctx', axis=0, tiled=True)]
    unnamed x79 -> x92, local copies, waits for them, and re-layouts: 22 us -> 39.8 us
    unnamed x14 -> x13, waiting for transfers between devices: 29.1 us -> 28.3 us
  transfers between devices with their start and end apart: 13 -> 15, of which waited for: 13 -> 14; matrix products, arithmetic and copies ran while one was open for 10% -> 12% of each run, Pallas kernels for 0% -> 0%
where the time goes in v1:
time: 911 us; the launch traced here: 904 us
  waiting for transfers between devices  604 us (66%)
  local copies, waits for them, and re-layouts  95.1 us (10%)
  matrix products  81.1 us (9%)
  blocking collectives  80.7 us (9%)
  other arithmetic  22.7 us (2%)
  between operations  17.2 us (2%)
    ppermute x3, waiting for transfers between devices, on_device(): lax.ppermute(ledger[-1], 'ctx', [(no, (no + 1) % n_shards) for no in rang...  158 us
    reduce_scatter x1, waiting for transfers between devices, on_device(): lax.psum_scatter(spread_grad, 'ctx', scatter_dimension=0, tiled=True)  95.1 us
    unnamed x2, blocking collectives  57.6 us
    reduce_scatter x1, waiting for transfers between devices, on_device(): lax.psum_scatter(grad_up_w.astype(jnp.bfloat16), 'wsh', scatter_dimension...  55.8 us
    reduce_scatter x1, waiting for transfers between devices, on_device(): lax.psum_scatter(grad_down_w.astype(jnp.bfloat16), 'wsh', scatter_dimensi...  55.3 us
    all_gather x1, waiting for transfers between devices, on_device(): lax.all_gather(up_weight, 'wsh', axis=0, tiled=True)  50.2 us
    all_gather x1, waiting for transfers between devices, on_device(): group_grads = lax.all_gather(grad_attended, 'ctx', axis=0, tiled=True)  42.9 us
    unnamed x92, local copies, waits for them, and re-layouts  39.8 us
  transfers between devices with their start and end apart: 15, of which 14 were waited for; matrix products, arithmetic and copies ran while one was open for 12% of the time, Pallas kernels for 0%

profile of v1, /device:TPU:0, one launch (start us, length us, event | category | flops | bytes accessed | tf_op | source)
XLA Modules:
  0.0 903.9 jit_solution(13826586290666783661)
XLA Ops:
  15.8 31.6 %all-reduce.18 = (bf16[768]{0:T(1024)(128)(2,1)S(1)}, bf16[768]{0:T(1024)(128)(2,1)S(1)}, bf16[768]{0:T(1024)(128)(2,1)S(1)}, bf16[768]{0:T(1024)(128)(2,1)S(1)}...) all-reduce(bf16[768]{0:T(1024)(128)(2,1)S(1)} %dynamic-update-slice, ...), channel_id=1, replica_groups=mesh['ctx'=4,'wsh'=8] {'wsh'}, use_global_device_ids=true, to_apply=%add.1 | all-reduce | flops 5376 | bytes 21504
  47.5 7.0 all-gather.7.cloned.1.call-done
  54.4 4.2 fusion.18
  60.2 52.8 %collective-permute-done = bf16[512,2304]{1,0:T(8,128)(2,1)S(1)} collective-permute-done((bf16[512,2304]{1,0:T(8,128)(2,1)S(1)}, bf16[512,2304]{1,0:T(8,128)(2,1)S(1)}, u32[]{:S(2)}, u32[]{:S(2)}) %collective-permute-start) | collective-permute-done | bytes 2359328 | tf_op jit(solution)/shard_map/ppermute | solution.py:114
  115.1 53.0 %collective-permute-done.1 = bf16[512,2304]{1,0:T(8,128)(2,1)} collective-permute-done((bf16[512,2304]{1,0:T(8,128)(2,1)S(1)}, bf16[512,2304]{1,0:T(8,128)(2,1)}, u32[]{:S(2)}, u32[]{:S(2)}) %collective-permute-start.1) | collective-permute-done | bytes 2359328 | tf_op jit(solution)/shard_map/ppermute | solution.py:114
  168.4 52.6 %collective-permute-done.2 = bf16[512,2304]{1,0:T(8,128)(2,1)} collective-permute-done((bf16[512,2304]{1,0:T(8,128)(2,1)}, bf16[512,2304]{1,0:T(8,128)(2,1)}, u32[]{:S(2)}, u32[]{:S(2)}) %collective-permute-start.2) | collective-permute-done | bytes 2359328 | tf_op jit(solution)/shard_map/ppermute | solution.py:114
  221.0 3.3 constant_dynamic-update-slice_fusion.7
  224.3 3.4 constant_dynamic-update-slice_fusion.6
  229.2 1.7 constant_dynamic-update-slice_fusion.4
  230.9 3.2 constant_dynamic-update-slice_fusion.3
  234.1 3.2 constant_dynamic-update-slice_fusion.2
  240.5 7.9 constant_dynamic-slice_fusion
  248.4 10.0 %gather_fusion = bf16[512,2304]{1,0:T(8,128)(2,1)S(1)} fusion(bf16[2048,2304]{1,0:T(8,128)(2,1)} %constant_dynamic-slice_fusion, s32[1024]{0:T(1024)S(1)} %pad_clamp_fusion), kind=kCustom, calls=%fused_computation | custom fusion | bytes 4720640 | tf_op jit(solution)/shard_map/jit(_take)/gather | solution.py:119
  266.2 2.3 add_convert_fusion.1
  268.6 4.7 scatter_custom_fusion
  274.5 13.2 %all-gather = bf16[8,1,384]{2,1,0:T(2,128)(2,1)S(1)} all-gather(bf16[1,1,384]{2,1,0:T(2,128)(2,1)S(1)} %reshape.219), channel_id=1, replica_groups=mesh['ctx'=4,'wsh'=8] {'wsh'}, dimensions={0}, use_global_device_ids=true | all-gather | bytes 6912 | tf_op jit(solution)/shard_map/all_gather | solution.py:87
  287.7 27.7 %reduce-scatter.9.cloned.1.call-done = bf16[512,768]{1,0:T(8,128)(2,1)} async-done(((bf16[2048,768]{1,0:T(8,128)(2,1)}), bf16[512,768]{1,0:T(8,128)(2,1)}) %reduce-scatter.9.cloned.1.call-update) | async-done | bytes 786448 | tf_op jit(solution)/shard_map/reduce_scatter | solution.py:143
  318.4 50.2 %all-gather.11.cloned.1.call-done = bf16[768,3072]{1,0:T(8,128)(2,1)} async-done(((bf16[96,3072]{1,0:T(8,128)(2,1)}), bf16[768,3072]{1,0:T(8,128)(2,1)}) %all-gather.11.cloned.1.call-update) | async-done | bytes 4718608 | tf_op jit(solution)/shard_map/all_gather | solution.py:86
  368.6 19.3 %fusion.2 = (bf16[512,3072]{1,0:T(8,128)(2,1)}, f32[512,3072]{1,0:T(8,128)}) fusion(f32[3072]{0:T(1024)S(1)} %bitcast.121, bf16[768,3072]{1,0:T(8,128)(2,1)} %all-gather.11.cloned.1.call-done, f32[768]{0:T(1024)S(1)} %convert_element_type.212, f32[768]{0:T(1024)S(1)} %convert_element_type.211, f32[512]{0:T(512)S(1)} %add_rsqrt_fusion.1, ...), kind=kOutput, calls=%fused_computation.8 | convolution fusion | flops 2522873856 | bytes 15751168 | tf_op jit(solution)/shard_map/dot_general | solution.py:148
  387.9 32.7 %all-gather.13.cloned.1.call-done = bf16[3072,768]{1,0:T(8,128)(2,1)} async-done(((bf16[384,768]{1,0:T(8,128)(2,1)}), bf16[3072,768]{1,0:T(8,128)(2,1)}) %all-gather.13.cloned.1.call-update) | async-done | bytes 4718608 | tf_op jit(solution)/shard_map/all_gather | solution.py:88
  420.6 6.3 fusion.87
  429.7 4.7 fusion.90
  434.4 3.2 multiply_reduce_fusion.1
  440.4 42.9 %all-gather.15.cloned.1.call-done = bf16[2048,768]{1,0:T(8,128)(2,1)} async-done(((bf16[512,768]{1,0:T(8,128)(2,1)}), bf16[2048,768]{1,0:T(8,128)(2,1)}) %all-gather.15.cloned.1.call-update) | async-done | bytes 3145744 | tf_op jit(solution)/shard_map/all_gather | solution.py:176
  483.3 5.5 gather_fusion.1
  488.8 3.2 convolution_convert_fusion.4
  492.1 2.3 copy.89
  494.4 2.4 reshape.158
  496.8 3.8 multiply_reduce_fusion
  508.9 4.3 copy.101
  513.2 10.6 %scatter_custom_fusion.1 = bf16[2048,2304]{1,0:T(8,128)(2,1)} fusion(s32[512]{0:T(512)S(1)} %bitcast.125, bf16[512,2304]{1,0:T(8,128)(2,1)} %copy.101, bf16[]{:T(256)} %constant.46.clone.1), kind=kCustom, calls=%fused_computation.34 | custom fusion | bytes 9437696 | tf_op jit(solution)/shard_map/scatter | solution.py:215
  523.9 95.1 %reduce-scatter.11.cloned.1.call-done = bf16[512,2304]{1,0:T(8,128)(2,1)} async-done(((bf16[2048,2304]{1,0:T(8,128)(2,1)}), bf16[512,2304]{1,0:T(8,128)(2,1)}) %reduce-scatter.11.cloned.1.call-update) | async-done | bytes 2359312 | tf_op jit(solution)/shard_map/reduce_scatter | solution.py:217
  619.0 5.5 fusion.19
  624.6 5.8 copy.107
  630.4 3.3 convolution_convert_fusion.3
  634.0 7.2 convolution_convert_fusion
  641.3 6.5 convolution_convert_fusion.1
  647.9 26.4 %reduce-scatter.19.cloned.1.call-done = bf16[96,2304]{1,0:T(8,128)(2,1)} async-done(((bf16[768,2304]{1,0:T(8,128)(2,1)}), bf16[96,2304]{1,0:T(8,128)(2,1)}) %reduce-scatter.19.cloned.1.call-update) | async-done | bytes 442384
  674.3 2.1 copy.108
  676.4 32.3 %reduce-scatter.13.cloned.1.call-done = bf16[96,768]{1,0:T(8,128)(2,1)} async-done(((bf16[768,768]{1,0:T(8,128)(2,1)}), bf16[96,768]{1,0:T(8,128)(2,1)}) %reduce-scatter.13.cloned.1.call-update) | async-done | bytes 147472 | tf_op jit(solution)/shard_map/reduce_scatter | solution.py:233
  708.7 55.3 %reduce-scatter.17.cloned.1.call-done = bf16[384,768]{1,0:T(8,128)(2,1)} async-done(((bf16[3072,768]{1,0:T(8,128)(2,1)}), bf16[384,768]{1,0:T(8,128)(2,1)}) %reduce-scatter.17.cloned.1.call-update) | async-done | bytes 589840 | tf_op jit(solution)/shard_map/reduce_scatter | solution.py:251
  764.0 55.8 %reduce-scatter.15.cloned.1.call-done = bf16[96,3072]{1,0:T(8,128)(2,1)} async-done(((bf16[768,3072]{1,0:T(8,128)(2,1)}), bf16[96,3072]{1,0:T(8,128)(2,1)}) %reduce-scatter.15.cloned.1.call-update) | async-done | bytes 589840 | tf_op jit(solution)/shard_map/reduce_scatter | solution.py:245
  822.8 26.0 %all-reduce.17 = (bf16[768]{0:T(1024)(128)(2,1)S(1)}, bf16[768]{0:T(1024)(128)(2,1)S(1)}, bf16[768]{0:T(1024)(128)(2,1)S(1)}, bf16[768]{0:T(1024)(128)(2,1)S(1)}...) all-reduce(bf16[768]{0:T(1024)(128)(2,1)S(1)} %dynamic-update-slice, ...), channel_id=1, replica_groups=mesh['ctx'=4,'wsh'=8] {'wsh'}, use_global_device_ids=true, to_apply=%add.7 | all-reduce | flops 9984 | bytes 39936
  849.5 9.9 %all-reduce.19 = (bf16[96]{0:T(256)(128)(2,1)S(1)}, bf16[96]{0:T(256)(128)(2,1)S(1)}, bf16[96]{0:T(256)(128)(2,1)S(1)}, bf16[96]{0:T(256)(128)(2,1)S(1)}, bf16[9...) all-reduce(bf16[96]{0:T(256)(128)(2,1)S(1)} %dynamic-slice.9, ...), channel_id=1, replica_groups=mesh['ctx'=4,'wsh'=8] {'ctx'}, use_global_device_ids=true, to_apply=%region_19.20 | all-reduce | flops 1152 | bytes 4608 | tf_op jit(solution)/shard_map/psum | solution.py:280
  865.3 6.4 add_bitcast_fusion
  871.7 18.6 %all-reduce.23.cloned.1.call-done = (bf16[96,2304]{0,1:T(8,128)(2,1)}, bf16[96,768]{1,0:T(8,128)(2,1)}, bf16[96,3072]{1,0:T(8,128)(2,1)}, bf16[384,768]{1,0:T(8,128)(2,1)}) async-done(((bf16[96,2304]{0,1:T(8,128)(2,1)}, bf16[96,768]{1,0:T(8,128)(2,1)}, bf16[96,3072]{1,0:T(8,128)(2,1)}, bf16[384,768]{1,0:T(8,128)(2,1)}), (bf16[96,2304]{0,1:T(8,128)(2,1)}, bf16[96,768]{1,0:T(8,128)(2,1)}, ...) | async-done | bytes 1769488 | tf_op jit(solution)/shard_map/psum | solution.py:279
  890.3 2.2 convert_element_type.247
  892.5 2.2 convert_element_type.250
  (178 shorter events, 52.7 us)
Async XLA Ops:
  7.2 47.2 %all-gather.7.cloned.1.call-start = ((), (), s32[]{:S(2)}) async-start(), calls=%async_computation.6 | async-start | bytes 3981312 | tf_op jit(solution)/shard_map/all_gather | solution.py:79
  7.9 258.3 %all-gather.9.cloned.1.call-start = ((), (), s32[]{:S(2)}) async-start(), calls=%async_computation.7 | async-start | bytes 1327104 | tf_op jit(solution)/shard_map/all_gather | solution.py:82
  47.5 120.8 %copy-start.18 = (s32[1,512]{1,0:T(1,128)S(1)}, s32[1,512]{1,0:T(1,128)}, u32[]{:S(2)}) copy-start(s32[1,512]{1,0:T(1,128)} %param.17) | copy-start | bytes 6148
  58.7 54.3 %collective-permute-start = (bf16[512,2304]{1,0:T(8,128)(2,1)S(1)}, bf16[512,2304]{1,0:T(8,128)(2,1)S(1)}, u32[]{:S(2)}, u32[]{:S(2)}) collective-permute-start(bf16[512,2304]{1,0:T(8,128)(2,1)S(1)} %fusion.18), channel_id=1, source_target_pairs={{0,8},{8,16},{16,24},{24,0},{1,9},{9,17},{17,25},{25,1},{2,10},{10... | collective-permute-start | bytes 7077896 | tf_op jit(solution)/shard_map/ppermute | solution.py:114
  113.0 1.5 copy-start.2
  114.6 53.6 %collective-permute-start.1 = (bf16[512,2304]{1,0:T(8,128)(2,1)S(1)}, bf16[512,2304]{1,0:T(8,128)(2,1)}, u32[]{:S(2)}, u32[]{:S(2)}) collective-permute-start(bf16[512,2304]{1,0:T(8,128)(2,1)S(1)} %collective-permute-done), channel_id=1, source_target_pairs={{0,8},{8,16},{16,24},{24,0},{1,9},{9,17},{17,25},{25,1},{2,10},{10... | collective-permute-start | bytes 7077896 | tf_op jit(solution)/shard_map/ppermute | solution.py:114
  168.1 52.9 %collective-permute-start.2 = (bf16[512,2304]{1,0:T(8,128)(2,1)}, bf16[512,2304]{1,0:T(8,128)(2,1)}, u32[]{:S(2)}, u32[]{:S(2)}) collective-permute-start(bf16[512,2304]{1,0:T(8,128)(2,1)} %collective-permute-done.1), channel_id=1, source_target_pairs={{0,8},{8,16},{16,24},{24,0},{1,9},{9,17},{17,25},{25,1},{2,10},{10... | collective-permute-start | bytes 7077896 | tf_op jit(solution)/shard_map/ppermute | solution.py:114
  168.2 147.2 %reduce-scatter.9.cloned.1.call-start = ((), (), s32[]{:S(2)}) async-start(), calls=%async_computation.8 | async-start | bytes 3932160 | tf_op jit(solution)/shard_map/reduce_scatter | solution.py:143
  224.3 3.4 copy-start.3
  260.2 1.8 copy-start.7
  261.5 1.1 copy-start.9
  262.7 1.8 copy-start.14
  263.5 2.0 copy-start
  266.1 2.4 copy-start.13
  268.6 5.9 copy-start.19
  268.6 46.8 %copy-start.4 = (bf16[1,512,768]{2,1,0:T(8,128)(2,1)S(1)}, bf16[1,512,768]{2,1,0:T(8,128)(2,1)}, u32[]{:S(2)}) copy-start(bf16[1,512,768]{2,1,0:T(8,128)(2,1)} %param.16) | copy-start | bytes 2359300
  273.3 95.3 %all-gather.11.cloned.1.call-start = ((), (), s32[]{:S(2)}) async-start(), calls=%async_computation.9 | async-start | bytes 5308416 | tf_op jit(solution)/shard_map/all_gather | solution.py:86
  273.8 146.8 %all-gather.13.cloned.1.call-start = ((), (), s32[]{:S(2)}) async-start(), calls=%async_computation.10 | async-start | bytes 5308416 | tf_op jit(solution)/shard_map/all_gather | solution.py:88
  274.4 208.9 %all-gather.15.cloned.1.call-start = ((), (), s32[]{:S(2)}) async-start(), calls=%async_computation.11 | async-start | bytes 3932160 | tf_op jit(solution)/shard_map/all_gather | solution.py:176
  315.4 53.2 %copy-start.5 = (bf16[512,768]{1,0:T(8,128)(2,1)S(1)}, bf16[512,768]{1,0:T(8,128)(2,1)}, u32[]{:S(2)}) copy-start(bf16[512,768]{1,0:T(8,128)(2,1)} %reduce-scatter.9.cloned.1.call-done) | copy-start | bytes 2359300
  420.6 6.6 copy-start.6
  420.6 8.0 copy-start.23
  427.2 2.4 copy-start.20
  428.0 6.4 slice-start
  428.6 5.8 copy-start.12
  429.7 4.8 slice-start.1
  434.4 3.3 copy-start.22
  437.7 1.1 copy-start.11
  440.4 178.7 %reduce-scatter.11.cloned.1.call-start = ((), (), s32[]{:S(2)}) async-start(), calls=%async_computation.12 | async-start | bytes 11796480 | tf_op jit(solution)/shard_map/reduce_scatter | solution.py:217
  496.8 3.8 copy-start.1
  496.8 3.8 copy-start.15
  502.0 1.2 copy-start.8
  503.2 1.2 copy-start.10
  523.8 150.5 %reduce-scatter.19.cloned.1.call-start = ((), (), s32[]{:S(2)}) async-start(), calls=%async_computation.16 | async-start | bytes 3981312
  630.4 78.3 %reduce-scatter.13.cloned.1.call-start = ((), (), s32[]{:S(2)}) async-start(), calls=%async_computation.13 | async-start | bytes 1327104 | tf_op jit(solution)/shard_map/reduce_scatter | solution.py:233
  633.7 130.3 %reduce-scatter.17.cloned.1.call-start = ((), (), s32[]{:S(2)}) async-start(), calls=%async_computation.15 | async-start | bytes 5308416 | tf_op jit(solution)/shard_map/reduce_scatter | solution.py:251
  641.3 178.5 %reduce-scatter.15.cloned.1.call-start = ((), (), s32[]{:S(2)}) async-start(), calls=%async_computation.14 | async-start | bytes 5308416 | tf_op jit(solution)/shard_map/reduce_scatter | solution.py:245
  647.8 174.6 %copy-start.21 = (bf16[96]{0:T(256)(128)(2,1)S(1)}, bf16[96]{0:T(256)(128)(2,1)}, u32[]{:S(2)}) copy-start(bf16[96]{0:T(256)(128)(2,1)} %param.30) | copy-start | bytes 580
  647.8 242.4 %all-reduce.23.cloned.1.call-start = ((), (), s32[]{:S(2)}) async-start(), calls=%async_computation.17 | async-start | bytes 3833856 | tf_op jit(solution)/shard_map/psum | solution.py:279
  890.3 4.4 copy-start.16
  890.3 5.6 copy-start.17
Sparse Core Ops, SparseCore 0:
  9.7 44.7 all-gather.6
  168.3 22.2 all-gather.8
  273.4 41.9 reduce-scatter.8
  316.9 51.6 all-gather.10
  370.1 50.5 all-gather.12
  440.5 42.7 all-gather.14
  524.0 95.0 reduce-scatter.10
  630.5 43.8 reduce-scatter.18
  677.3 31.3 reduce-scatter.12
  711.0 53.0 reduce-scatter.16
  766.4 53.3 reduce-scatter.14
  824.1 66.0 all-reduce.22
